TPU v7x, 256 devices: a whole 4x4x8 slice. The times are simulated.
256 devices in a mesh: dp: 16 (over x, y), tensor: 16 (over z, core).
Axes of the slice: x: 4, y: 4, z: 8, core: 2. Of those that a mesh axis runs over, the one named last changes fastest.
Arguments:
- tokens: bfloat16 [8192, 8192], P(('dp', 'tensor')), may hold values from -6 to 6
- w_query: bfloat16 [8192, 8192], P(None, 'tensor'), may hold values from -0.0625 to 0.0625
- cotangent: bfloat16 [8192, 8192], P('dp', 'tensor'), may hold values from -6 to 6
- task_embed: bfloat16 [128, 1024], replicated, may hold values from -6 to 6
- w_hidden: bfloat16 [1024, 512], P(None, 'tensor'), may hold values from -0.1875 to 0.1875
- head_a: bfloat16 [512, 16, 8192], P(None, 'dp', 'tensor'), may hold values from -0.0234375 to 0.0234375
- head_b: bfloat16 [512, 16, 8192], P(None, 'dp', 'tensor'), may hold values from -0.0234375 to 0.0234375
- block_task: int32 [16], replicated, may hold values from 0 to 127
Outputs:
- output: bfloat16 [8192, 8192], P('dp', 'tensor')
- grad_tokens: bfloat16 [8192, 8192], P(('dp', 'tensor'))
- grad_head_a: bfloat16 [512, 16, 8192], P(None, 'dp', 'tensor')
- grad_head_b: bfloat16 [512, 16, 8192], P(None, 'dp', 'tensor')
All inputs are finite; a program needn't handle non-finite values.
Results may differ from a plain program's by a relative error of at most 0.0077.
Values may be sent and summed in bfloat16 or wider, within the bound.
No kernel may reach another device: no remote copies, remote signals or barrier semaphores. Data moves between devices by JAX's collectives and lax.ppermute only.
A program may use at most 128 MiB of HBM per device.

v0:
```python
import jax
import jax.numpy as jnp
from jax import lax
from jax.sharding import PartitionSpec as P


def local(tokens, w_query, cotangent, task_embed, w_hidden, head_a, head_b, block_task):
    single_float = jnp.float32
    brain_half_float = jnp.bfloat16
    n_groups = lax.axis_size("dp")
    n_shards = lax.axis_size("tensor")
    shard = lax.axis_index("tensor")
    group = lax.axis_index("dp")
    hid_count, rank_rows, width = head_a.shape
    ntasks = task_embed.shape[0]
    blocks = block_task.shape[0]
    per_group = blocks // n_groups
    hid_part = jax.nn.silu(
        jnp.dot(task_embed, w_hidden, preferred_element_type=single_float)
    ).astype(brain_half_float)
    hidden = lax.all_gather(hid_part, "tensor", axis=1, tiled=True)
    flat_a = head_a.reshape(hid_count, rank_rows * width)
    flat_b = head_b.reshape(hid_count, rank_rows * width)
    mine = lax.dynamic_slice_in_dim(block_task, group * per_group, per_group)
    task_ids = jnp.arange(ntasks, dtype=jnp.int32)
    gen_a = (
        jnp.dot(hidden, flat_a, preferred_element_type=single_float)
        .astype(brain_half_float)
        .reshape(ntasks, rank_rows, width)
    )
    gen_b = (
        jnp.dot(hidden, flat_b, preferred_element_type=single_float)
        .astype(brain_half_float)
        .reshape(ntasks, rank_rows, width)
    )
    all_tasks_down, all_tasks_up = (
        lax.all_gather(gen_a, "dp", axis=1, tiled=True),
        lax.all_gather(gen_b, "dp", axis=1, tiled=True),
    )
    task_selector = (mine[:, None] == task_ids[None, :]).astype(brain_half_float)
    adapter_down_weight = jnp.einsum(
        "yg,ghi->yhi", task_selector, all_tasks_down, preferred_element_type=single_float
    ).astype(brain_half_float)
    adapter_up_weight = jnp.einsum(
        "yg,ghi->yhi", task_selector, all_tasks_up, preferred_element_type=single_float
    ).astype(brain_half_float)
    rank = adapter_down_weight.shape[1]
    whole = lax.all_gather(tokens, "tensor", axis=0, tiled=True)
    rows_all, model_width = whole.shape
    block = rows_all // per_group
    rows_dev = rows_all // n_shards
    block_inputs = whole.reshape(per_group, block, model_width)
    input_columns = lax.dynamic_slice_in_dim(block_inputs, shard * width, width, 2)
    frozen_output = jnp.dot(whole, w_query, preferred_element_type=single_float)
    down_portion = jnp.einsum(
        "grs,gps->grp", input_columns, adapter_down_weight, preferred_element_type=single_float
    )
    down_projection = lax.psum(down_portion, "tensor")
    down_low_rank = down_projection.astype(brain_half_float)
    low_rank_update = jnp.einsum(
        "elm,emn->eln", down_low_rank, adapter_up_weight, preferred_element_type=single_float
    ).reshape(rows_all, width)
    output = (frozen_output + low_rank_update).astype(brain_half_float)
    block_output_grads = cotangent.reshape(per_group, block, width)
    backward_portion = jnp.einsum(
        "grs,gps->grp", block_output_grads, adapter_up_weight, preferred_element_type=single_float
    )
    backward_input = lax.psum(backward_portion, "tensor")
    backward_low_rank = backward_input.astype(brain_half_float)
    grad_sum = lax.psum_scatter(
        lax.dot_general(
            cotangent, w_query, (((1,), (1,)), ((), ())), preferred_element_type=single_float
        ),
        "tensor",
        scatter_dimension=0,
        tiled=True,
    )
    full_a = lax.all_gather(adapter_down_weight, "tensor", axis=2, tiled=True)
    first = shard * rows_dev
    which = first // block
    a_here = lax.dynamic_index_in_dim(full_a, which, 0, keepdims=False)
    back_rows = lax.dynamic_slice_in_dim(
        backward_low_rank.reshape(rows_all, rank), first, rows_dev, 0
    )
    grad_sum = grad_sum + jnp.dot(back_rows, a_here, preferred_element_type=single_float)
    grad_tokens = grad_sum.astype(brain_half_float)
    scale_average = 1.0 / block
    down_gradient = (
        jnp.einsum(
            "evr,evx->erx", backward_low_rank, input_columns, preferred_element_type=single_float
        )
        * scale_average
    ).astype(brain_half_float)
    up_gradient = (
        jnp.einsum(
            "evr,evx->erx", down_low_rank, block_output_grads, preferred_element_type=single_float
        )
        * scale_average
    ).astype(brain_half_float)
    task_down_weight = jnp.einsum(
        "xh,xui->hui", task_selector, down_gradient, preferred_element_type=single_float
    )
    task_up_weight = jnp.einsum(
        "xh,xui->hui", task_selector, up_gradient, preferred_element_type=single_float
    )
    own_a, own_b = (
        lax.psum_scatter(
            task_down_weight.astype(jnp.bfloat16), "dp", scatter_dimension=1, tiled=True
        ).astype(jnp.float32),
        lax.psum_scatter(
            task_up_weight.astype(jnp.bfloat16), "dp", scatter_dimension=1, tiled=True
        ).astype(jnp.float32),
    )
    hid_f = hidden.astype(single_float)
    head_grad_a = lax.dot_general(
        hid_f,
        own_a.reshape(ntasks, rank_rows * width),
        (((0,), (0,)), ((), ())),
        precision=lax.Precision.HIGHEST,
    )
    head_grad_b = lax.dot_general(
        hid_f,
        own_b.reshape(ntasks, rank_rows * width),
        (((0,), (0,)), ((), ())),
        precision=lax.Precision.HIGHEST,
    )
    grad_head_a = head_grad_a.reshape(hid_count, rank_rows, width).astype(brain_half_float)
    grad_head_b = head_grad_b.reshape(hid_count, rank_rows, width).astype(brain_half_float)
    return (output, grad_tokens, grad_head_a, grad_head_b)


def solution(mesh):
    return jax.shard_map(
        local,
        mesh=mesh,
        in_specs=(
            P(("dp", "tensor"), None),
            P(None, "tensor"),
            P("dp", "tensor"),
            P(),
            P(None, "tensor"),
            P(None, "dp", "tensor"),
            P(None, "dp", "tensor"),
            P(),
        ),
        out_specs=(
            P("dp", "tensor"),
            P(("dp", "tensor"), None),
            P(None, "dp", "tensor"),
            P(None, "dp", "tensor"),
        ),
        check_vma=False,
    )
```

profile of v0, /device:TPU:2, one launch (start us, length us, event | category | flops | bytes accessed | tf_op | source)
XLA Modules:
  0.0 520.4 jit_solution(2591239751184445774)
XLA Ops:
  7.2 0.0 copy-start
  7.2 0.0 all-gather.9.cloned.1.call-start
  7.2 1.2 multiply_convert_fusion.2
  8.4 20.3 %all_gather.16 = bf16[128,512]{0,1:T(8,128)(2,1)S(1)} all-gather(bf16[128,32]{0,1:T(8,128)(2,1)S(1)} %multiply_convert_fusion.2), channel_id=1, replica_groups=mesh['dp'=16,'tensor'=16] {'tensor'}, dimensions={1}, use_global_device_ids=true | all-gather | bytes 139264 | tf_op jit(solution)/shard_map/all_gather | solution.py:21
  28.8 2.0 convolution_convert_fusion.3
  30.7 0.0 all-gather.9.cloned.1.call-update
  30.7 0.0 all-gather.11.cloned.1.call-start
  30.8 2.0 convolution_convert_fusion.2
  32.7 0.0 all-gather.11.cloned.1.call-update
  32.8 0.0 all-gather.7.cloned.1.call-start
  32.8 0.7 all-gather.7.cloned.1.call-update
  33.5 0.0 reduce-scatter.10.cloned.1.call-start
  33.6 1.2 dynamic_slice.11
  34.8 0.6 fusion.29
  35.5 45.3 %all-gather.9.cloned.1.call-done = bf16[128,8192]{1,0:T(8,128)(2,1)} async-done(((bf16[128,512]{1,0:T(8,128)(2,1)}), bf16[128,8192]{1,0:T(8,128)(2,1)}) %all-gather.9.cloned.1.call-update) | async-done | bytes 2097168 | tf_op jit(solution)/shard_map/all_gather | solution.py:37
  80.7 2.6 fusion.4
  83.3 51.8 %all-gather.11.cloned.1.call-done = bf16[128,8192]{1,0:T(8,128)(2,1)} async-done(((bf16[128,512]{1,0:T(8,128)(2,1)}), bf16[128,8192]{1,0:T(8,128)(2,1)}) %all-gather.11.cloned.1.call-update) | async-done | bytes 2097168 | tf_op jit(solution)/shard_map/all_gather | solution.py:38
  135.2 2.6 fusion.1
  137.8 0.0 copy-done
  137.8 0.2 convolution_bitcast_fusion
  138.0 54.6 %all-gather.7.cloned.1.call-done = bf16[512,8192]{1,0:T(8,128)(2,1)} async-done(((bf16[32,8192]{1,0:T(8,128)(2,1)}), bf16[512,8192]{1,0:T(8,128)(2,1)}) %all-gather.7.cloned.1.call-update) | async-done | bytes 8388624 | tf_op jit(solution)/shard_map/all_gather | solution.py:48
  192.6 1.3 convolution_bitcast_fusion.1
  193.9 46.9 %all-reduce.2 = (bf16[1,512,16]{1,2,0:T(8,128)(2,1)S(1)}, bf16[1,512,16]{1,2,0:T(8,128)(2,1)S(1)}) all-reduce(f32[1,512,16]{1,2,0:T(8,128)S(1)} %convolution_bitcast_fusion.1, f32[1,512,16]{1,2,0:T(8,128)S(1)} %convolution_bitcast_fusion), channel_id=1, replica_groups=mesh['dp'=16,'tensor'=16] {'tensor'}, use_global_device_ids=true, to_apply=%region_0.1 | all-reduce | flops 16384 | bytes 98304 | tf_op jit(solution)/shard_map/psum | solution.py:58
  240.8 0.2 fusion.13
  240.9 1.2 fusion.11
  242.2 3.5 multiply_convert_fusion
  245.6 0.0 reduce-scatter.10.cloned.1.call-update
  245.7 0.0 reduce-scatter.12.cloned.1.call-start
  245.7 0.5 reduce-scatter.12.cloned.1.call-update
  246.3 0.0 reduce-scatter.8.cloned.1.call-start
  246.3 11.6 %fusion.36 = f32[512,8192]{1,0:T(8,128)} fusion(bf16[512,512]{1,0:T(8,128)(2,1)S(1)} %copy-done, bf16[8192,512]{1,0:T(8,128)(2,1)} %param.9), kind=kOutput, calls=%fused_computation.52 | convolution fusion | flops 4294967296 | bytes 25690112 | tf_op jit(solution)/shard_map/dot_general | solution.py:71
  257.9 0.0 reduce-scatter.8.cloned.1.call-update
  257.9 14.9 %all-gather.2 = bf16[16,8192]{1,0:T(8,128)(2,1)S(1)} all-gather(bf16[16,512]{1,0:T(8,128)(2,1)S(1)} %bitcast.73), channel_id=4, replica_groups=mesh['dp'=16,'tensor'=16] {'tensor'}, dimensions={1}, use_global_device_ids=true | all-gather | bytes 278528 | tf_op jit(solution)/shard_map/all_gather | solution.py:78
  272.8 9.5 %fusion.35 = f32[512,512]{1,0:T(8,128)S(1)} fusion(bf16[512,8192]{1,0:T(8,128)(2,1)} %all-gather.7.cloned.1.call-done, bf16[8192,512]{1,0:T(8,128)(2,1)} %param.9), kind=kOutput, calls=%fused_computation.51 | convolution fusion | flops 4294967296 | bytes 17825792 | tf_op jit(solution)/shard_map/dot_general | solution.py:54
  282.3 1.1 fusion.7
  283.4 42.0 %reduce-scatter.10.cloned.1.call-done = bf16[128,1,512]{2,0,1:T(8,128)(2,1)} async-done(((bf16[128,16,512]{2,0,1:T(8,128)(2,1)}), bf16[128,1,512]{2,0,1:T(8,128)(2,1)}) %reduce-scatter.10.cloned.1.call-update) | async-done | bytes 131088
  325.4 2.0 fusion.8
  327.4 81.0 %reduce-scatter.12.cloned.1.call-done = bf16[128,1,512]{2,0,1:T(8,128)(2,1)} async-done(((bf16[128,16,512]{2,0,1:T(8,128)(2,1)}), bf16[128,1,512]{2,0,1:T(8,128)(2,1)}) %reduce-scatter.12.cloned.1.call-update) | async-done | bytes 131088
  408.5 2.0 fusion.9
  410.4 100.7 %reduce-scatter.8.cloned.1.call-done = f32[32,8192]{1,0:T(8,128)} async-done(((f32[512,8192]{1,0:T(8,128)}), f32[32,8192]{1,0:T(8,128)}) %reduce-scatter.8.cloned.1.call-update) | async-done | bytes 1048592 | tf_op jit(solution)/shard_map/reduce_scatter | solution.py:70
  511.1 2.4 fusion
  (1 shorter events, 0.0 us)
Async XLA Ops:
  7.2 130.6 %copy-start = (bf16[512,512]{1,0:T(8,128)(2,1)S(1)}, bf16[512,512]{1,0:T(8,128)(2,1)}, u32[]{:S(2)}) copy-start(bf16[512,512]{1,0:T(8,128)(2,1)} %param.10) | copy-start | bytes 1572868
  7.2 73.5 %all-gather.9.cloned.1.call-start = ((), (), s32[]{:S(2)}) async-start(), calls=%async_computation.5 | async-start | bytes 2228224 | tf_op jit(solution)/shard_map/all_gather | solution.py:37
  30.7 104.4 %all-gather.11.cloned.1.call-start = ((), (), s32[]{:S(2)}) async-start(), calls=%async_computation.6 | async-start | bytes 2228224 | tf_op jit(solution)/shard_map/all_gather | solution.py:38
  32.8 159.8 %all-gather.7.cloned.1.call-start = ((), (), s32[]{:S(2)}) async-start(), calls=%async_computation.3 | async-start | bytes 8912896 | tf_op jit(solution)/shard_map/all_gather | solution.py:48
  33.5 291.9 %reduce-scatter.10.cloned.1.call-start = ((), (), s32[]{:S(2)}) async-start(), calls=%async_computation.7 | async-start | bytes 2228224
  245.7 162.8 %reduce-scatter.12.cloned.1.call-start = ((), (), s32[]{:S(2)}) async-start(), calls=%async_computation.8 | async-start | bytes 2228224
  246.3 264.9 %reduce-scatter.8.cloned.1.call-start = ((), (), s32[]{:S(2)}) async-start(), calls=%async_computation.4 | async-start | bytes 17825792 | tf_op jit(solution)/shard_map/reduce_scatter | solution.py:70
Sparse Core Ops, SparseCore 0:
  30.9 49.8 all-gather.8
  83.7 51.4 all-gather.10
  137.0 55.5 all-gather.6
  245.8 79.6 reduce-scatter.9
  328.8 79.5 reduce-scatter.11
  410.9 100.2 reduce-scatter.7
where the time goes:
time: 521 us; the launch traced here: 520 us
  waiting for transfers between devices  377 us (72%)
  blocking collectives  82.1 us (16%)
  matrix products  41.8 us (8%)
  between operations  14.2 us (3%)
    unnamed x8, waiting for transfers between devices  124 us
    reduce_scatter x1, waiting for transfers between devices, local(): lax.psum_scatter(lax.dot_general(cotangent, w_query, (((1,), (1,)), ((),...  101 us
    all_gather x1, waiting for transfers between devices, local(): whole = lax.all_gather(tokens, 'tensor', axis=0, tiled=True)  54.6 us
    all_gather x1, waiting for transfers between devices, local(): lax.all_gather(gen_b, 'dp', axis=1, tiled=True)  51.8 us
    psum x1, blocking collectives, local(): down_projection = lax.psum(down_portion, 'tensor')  46.9 us
    all_gather x1, waiting for transfers between devices, local(): lax.all_gather(gen_a, 'dp', axis=1, tiled=True)  45.3 us
    all_gather x1, blocking collectives, local(): hidden = lax.all_gather(hid_part, 'tensor', axis=1, tiled=True)  20.3 us
    all_gather x1, blocking collectives, local(): full_a = lax.all_gather(adapter_down_weight, 'tensor', axis=2, tiled=True)  14.9 us
  transfers between devices with their start and end apart: 6, of which 6 were waited for; matrix products, arithmetic and copies ran while one was open for 7% of the time, Pallas kernels for 0%

commit v1 on v0

v1 whole, which is shorter than its diff:
```python
import jax
import jax.numpy as jnp
from jax import lax
from jax.sharding import PartitionSpec as P

F32 = jnp.float32
BF16 = jnp.bfloat16


def dot(a, b, ca, cb):
    return lax.dot_general(a, b, (((ca,), (cb,)), ((), ())), preferred_element_type=F32)


def local(tokens, w_query, cotangent, task_embed, w_hidden, head_a, head_b, block_task):
    shard = lax.axis_index("tensor")
    hid_count, rank_rows, width = head_a.shape
    ntasks = task_embed.shape[0]
    blocks = block_task.shape[0]
    rows = cotangent.shape[0]
    whole = lax.all_gather(tokens, "tensor", axis=0, tiled=True)
    hid_part = jax.nn.silu(dot(task_embed, w_hidden, 1, 0)).astype(BF16)
    pick = (block_task[:, None] == jnp.arange(ntasks, dtype=jnp.int32)[None, :]).astype(BF16)
    hid_part = dot(pick, hid_part, 1, 0).astype(BF16)
    hidden = lax.all_gather(hid_part, "tensor", axis=1, tiled=True)
    gen_a = dot(hidden, head_a.reshape(hid_count, width), 1, 0).astype(BF16)
    gen_b = dot(hidden, head_b.reshape(hid_count, width), 1, 0).astype(BF16)
    factors = lax.all_to_all(jnp.stack([gen_a, gen_b], 1), "dp", 0, 0, tiled=True)
    down_w = factors[:, 0]
    up_w = factors[:, 1]
    rank = down_w.shape[0]
    back_part = dot(up_w, cotangent, 1, 1).astype(BF16)
    both = lax.all_gather(jnp.concatenate([down_w, back_part], 0), "tensor", axis=0, tiled=False)
    back_low = both[:, rank:].astype(F32).sum(0).astype(BF16)
    full_a = both[:, :rank].transpose(1, 0, 2).reshape(rank, -1)
    grad_part = (dot(cotangent, w_query, 1, 1) + dot(back_part, full_a, 0, 0)).astype(BF16)
    grad_tokens = lax.psum_scatter(grad_part, "tensor", scatter_dimension=0, tiled=True)
    down_low = dot(whole, full_a, 1, 1).astype(BF16)
    columns = lax.dynamic_slice_in_dim(whole, shard * width, width, 1)
    scale = 1.0 / rows
    grad_a = (dot(back_low, columns, 1, 0) * scale).astype(BF16)
    grad_b = (dot(down_low, cotangent, 0, 0) * scale).astype(BF16)
    own = lax.all_to_all(jnp.stack([grad_a, grad_b], 1), "dp", 0, 0, tiled=True)
    head_grad_a = dot(hidden, own[:, 0], 0, 0).astype(BF16).reshape(hid_count, rank_rows, width)
    head_grad_b = dot(hidden, own[:, 1], 0, 0).astype(BF16).reshape(hid_count, rank_rows, width)
    output = (dot(whole, w_query, 1, 0) + dot(down_low, up_w, 1, 0)).astype(BF16)
    return (output, grad_tokens, head_grad_a, head_grad_b)


def solution(mesh):
    return jax.shard_map(
        local,
        mesh=mesh,
        in_specs=(
            P(("dp", "tensor"), None),
            P(None, "tensor"),
            P("dp", "tensor"),
            P(),
            P(None, "tensor"),
            P(None, "dp", "tensor"),
            P(None, "dp", "tensor"),
            P(),
        ),
        out_specs=(
            P("dp", "tensor"),
            P(("dp", "tensor"), None),
            P(None, "dp", "tensor"),
            P(None, "dp", "tensor"),
        ),
        check_vma=False,
    )
```

time: 521 us -> 159 us (0.31)
  waiting for transfers between devices: 377 us -> 42.3 us
  blocking collectives: 82.1 us -> 38.5 us
  starting transfers between devices: 0.24 us -> 14.8 us
  matrix products: 41.8 us -> 47.3 us
    unnamed x8 -> x2, waiting for transfers between devices: 124 us -> 0.7 us
    all_gather x2 -> x0, waiting for transfers between devices: 97.1 us -> none  [the longest x1 51.8 us: local(): lax.all_gather(gen_b, 'dp', axis=1, tiled=True)]
    reduce_scatter x1, waiting for transfers between devices: 101 us -> 41.6 us  [local(): lax.psum_scatter(grad_part, 'tensor', scatter_dimension=0, tiled=True)]
    all_gather x1, waiting for transfers between devices: 54.6 us -> 0.02 us  [local(): whole = lax.all_gather(tokens, 'tensor', axis=0, tiled=True)]
    psum x1 -> x0, blocking collectives: 46.9 us -> none  [local(): down_projection = lax.psum(down_portion, 'tensor')]
    all_to_all x0 -> x2, starting transfers between devices: none -> 14.7 us  [the longest x1 7.48 us: local(): lax.all_to_all(jnp.stack([gen_a, gen_b], 1), 'dp', 0, 0, tiled=True)]
    dot_general x15 -> x13, matrix products: 41.8 us -> 47.3 us  [dot(): lax.dot_general(a, b, (((ca,), (cb,)), ((), ())), preferred_element_type=...]
  transfers between devices with their start and end apart: 6 -> 4, of which waited for: 6 -> 1; matrix products, arithmetic and copies ran while one was open for 7% -> 31% of each run, Pallas kernels for 0% -> 0%
where the time goes in v1:
time: 159 us
  matrix products  47.3 us (30%)
  waiting for transfers between devices  42.3 us (27%)
  blocking collectives  38.5 us (24%)
  starting transfers between devices  14.8 us (9%)
  between operations  14.1 us (9%)
  local copies, waits for them, and re-layouts  1.6 us (1%)
    dot_general x13, matrix products, dot(): lax.dot_general(a, b, (((ca,), (cb,)), ((), ())), preferred_element_type=...  47.3 us
    reduce_scatter x1, waiting for transfers between devices, local(): lax.psum_scatter(grad_part, 'tensor', scatter_dimension=0, tiled=True)  41.6 us
    all_gather x1, blocking collectives, local(): hidden = lax.all_gather(hid_part, 'tensor', axis=1, tiled=True)  20.1 us
    all_gather x1, blocking collectives, local(): lax.all_gather(jnp.concatenate([down_w, back_part], 0), 'tensor', axis=0,...  18.4 us
    all_to_all x1, starting transfers between devices, local(): lax.all_to_all(jnp.stack([gen_a, gen_b], 1), 'dp', 0, 0, tiled=True)  7.48 us
    all_to_all x1, starting transfers between devices, local(): own = lax.all_to_all(jnp.stack([grad_a, grad_b], 1), 'dp', 0, 0, tiled=True)  7.27 us
  transfers between devices with their start and end apart: 4, of which 1 were waited for; matrix products, arithmetic and copies ran while one was open for 31% of the time, Pallas kernels for 0%

profile of v1, /device:TPU:2, one launch (start us, length us, event | category | flops | bytes accessed | tf_op | source)
XLA Modules:
  0.0 158.7 jit_solution(4252465929384589923)
XLA Ops:
  7.2 0.0 copy-start
  7.2 0.0 all-gather.4.cloned.1.call-start
  7.2 0.7 all-gather.4.cloned.1.call-update
  7.9 1.3 fusion.9
  9.2 20.1 %all-gather.1 = bf16[16,32,16]{1,2,0:T(8,128)(2,1)S(1)} all-gather(bf16[1,32,16]{1,2,0:T(8,128)(2,1)S(1)} %fusion.9), channel_id=1, replica_groups=mesh['dp'=16,'tensor'=16] {'tensor'}, dimensions={0}, use_global_device_ids=true | all-gather | bytes 17408 | tf_op jit(solution)/shard_map/all_gather | solution.py:24
  29.3 0.1 reshape.31
  29.5 1.2 fusion.6
  30.7 1.2 fusion.5
  31.9 0.7 copy.20
  32.6 7.5 %all-to-all-start = ((bf16[16,2,512]{2,1,0:T(2,128)(2,1)}), bf16[16,2,512]{2,1,0:T(2,128)(2,1)S(1)}, u32[]{:S(2)}, u32[]{:S(2)}) async-start(bf16[16,2,512]{2,1,0:T(2,128)(2,1)} %copy.20), calls=%async_computation | async-start | bytes 65536 | tf_op jit(solution)/shard_map/all_to_all | solution.py:27
  40.1 0.0 reduce-scatter.2.cloned.1.call-start
  40.1 0.0 copy-done
  40.1 11.9 %fusion.21 = f32[512,8192]{1,0:T(8,128)} fusion(bf16[512,512]{1,0:T(8,128)(2,1)S(1)} %copy-done, bf16[8192,512]{1,0:T(8,128)(2,1)} %param.9), kind=kOutput, calls=%fused_computation.41 | convolution fusion | flops 4294967296 | bytes 25690112 | tf_op jit(solution)/shard_map/dot_general | solution.py:11
  52.0 0.0 all-to-all-done
  52.0 0.2 convolution_convert_fusion.3
  52.3 18.4 %all-gather = bf16[512,512]{1,0:T(8,128)(2,1)S(1)} all-gather(bf16[32,512]{1,0:T(8,128)(2,1)S(1)} %pad_maximum_fusion.1), channel_id=2, replica_groups=mesh['dp'=16,'tensor'=16] {'tensor'}, dimensions={0}, use_global_device_ids=true | all-gather | bytes 557056 | tf_op jit(solution)/shard_map/all_gather | solution.py:32
  70.7 11.4 %add_convert_fusion = bf16[512,8192]{1,0:T(8,128)(2,1)} fusion(f32[512,8192]{1,0:T(8,128)} %fusion.21, bf16[16,512]{1,0:T(8,128)(2,1)S(1)} %convolution_convert_fusion.3, bf16[16,8192]{1,0:T(8,128)(2,1)S(1)} %bitcast.61), kind=kOutput, calls=%fused_computation | convolution fusion | flops 142606336 | bytes 25444352 | tf_op jit(solution)/shard_map/dot_general | solution.py:11
  82.1 0.0 reduce-scatter.2.cloned.1.call-update
  82.1 0.0 all-gather.4.cloned.1.call-done
  82.2 1.2 fusion.8
  83.4 5.7 %convolution_convert_fusion.2 = bf16[16,512]{1,0:T(8,128)(2,1)S(1)} fusion(bf16[16,8192]{1,0:T(8,128)(2,1)S(1)} %bitcast.62, bf16[512,8192]{1,0:T(8,128)(2,1)} %all-gather.4.cloned.1.call-done), kind=kOutput, calls=%fused_computation.9 | convolution fusion | flops 134225920 | bytes 8667136 | tf_op jit(solution)/shard_map/dot_general | solution.py:11
  89.0 0.2 fusion.7
  89.2 0.7 copy.24
  89.9 7.3 %all-to-all-start.1 = ((bf16[16,2,512]{2,1,0:T(2,128)(2,1)}), bf16[16,2,512]{2,1,0:T(2,128)(2,1)S(1)}, u32[]{:S(2)}, u32[]{:S(2)}) async-start(bf16[16,2,512]{2,1,0:T(2,128)(2,1)} %copy.24), calls=%async_computation.2 | async-start | bytes 65536 | tf_op jit(solution)/shard_map/all_to_all | solution.py:42
  97.2 9.7 %fusion.20 = f32[512,512]{1,0:T(8,128)S(1)} fusion(bf16[512,8192]{1,0:T(8,128)(2,1)} %all-gather.4.cloned.1.call-done, bf16[8192,512]{1,0:T(8,128)(2,1)} %param.9), kind=kOutput, calls=%fused_computation.40 | convolution fusion | flops 4294967296 | bytes 17825792 | tf_op jit(solution)/shard_map/dot_general | solution.py:11
  106.9 1.1 fusion
  108.0 0.0 all-to-all-done.1
  108.1 1.1 fusion.2
  109.2 1.1 fusion.1
  110.3 41.6 %reduce-scatter.2.cloned.1.call-done = bf16[32,8192]{1,0:T(8,128)(2,1)} async-done(((bf16[512,8192]{1,0:T(8,128)(2,1)}), bf16[32,8192]{1,0:T(8,128)(2,1)}) %reduce-scatter.2.cloned.1.call-update) | async-done | bytes 524304 | tf_op jit(solution)/shard_map/reduce_scatter | solution.py:36
  (9 shorter events, 0.2 us)
Async XLA Ops:
  7.2 32.9 %copy-start = (bf16[512,512]{1,0:T(8,128)(2,1)S(1)}, bf16[512,512]{1,0:T(8,128)(2,1)}, u32[]{:S(2)}) copy-start(bf16[512,512]{1,0:T(8,128)(2,1)} %param.10) | copy-start | bytes 1572868
  7.2 75.0 %all-gather.4.cloned.1.call-start = ((), (), s32[]{:S(2)}) async-start(), calls=%async_computation.3 | async-start | bytes 8912896 | tf_op jit(solution)/shard_map/all_gather | solution.py:20
  32.6 19.4 %all-to-all-start = ((bf16[16,2,512]{2,1,0:T(2,128)(2,1)}), bf16[16,2,512]{2,1,0:T(2,128)(2,1)S(1)}, u32[]{:S(2)}, u32[]{:S(2)}) async-start(bf16[16,2,512]{2,1,0:T(2,128)(2,1)} %copy.20), calls=%async_computation | async-start | bytes 65536 | tf_op jit(solution)/shard_map/all_to_all | solution.py:27
  40.1 111.8 %reduce-scatter.2.cloned.1.call-start = ((), (), s32[]{:S(2)}) async-start(), calls=%async_computation.4 | async-start | bytes 8912896 | tf_op jit(solution)/shard_map/reduce_scatter | solution.py:36
  89.9 18.1 %all-to-all-start.1 = ((bf16[16,2,512]{2,1,0:T(2,128)(2,1)}), bf16[16,2,512]{2,1,0:T(2,128)(2,1)S(1)}, u32[]{:S(2)}, u32[]{:S(2)}) async-start(bf16[16,2,512]{2,1,0:T(2,128)(2,1)} %copy.24), calls=%async_computation.2 | async-start | bytes 65536 | tf_op jit(solution)/shard_map/all_to_all | solution.py:42
Sparse Core Ops, SparseCore 0:
  9.8 61.5 all-gather.3
  82.3 69.5 reduce-scatter.1

commit v2 on v1

v2 whole, which is shorter than its diff:
```python
import jax
import jax.numpy as jnp
from jax import lax
from jax.sharding import Mesh
from jax.sharding import PartitionSpec as P

F32 = jnp.float32
BF16 = jnp.bfloat16
AXIS = ("z", "core")


def dot(a, b, ca, cb):
    return lax.dot_general(a, b, (((ca,), (cb,)), ((), ())), preferred_element_type=F32)


def gather_small(x):
    n = lax.axis_size(AXIS)
    return lax.all_to_all(jnp.broadcast_to(x[None], (n,) + x.shape), AXIS, 0, 0, tiled=True)


def local(tokens, w_query, cotangent, task_embed, w_hidden, head_a, head_b, block_task):
    shards = lax.axis_size(AXIS)
    chips = shards // 2
    shard = lax.axis_index(AXIS)
    hid_count, rank_rows, width = head_a.shape
    ntasks = task_embed.shape[0]
    rows = cotangent.shape[0]
    part = rows // shards

    whole = lax.all_gather(tokens, AXIS, axis=0, tiled=True)
    hid_part = jax.nn.silu(dot(task_embed, w_hidden, 1, 0)).astype(BF16)
    pick = (block_task[:, None] == jnp.arange(ntasks, dtype=jnp.int32)[None, :]).astype(BF16)
    hid_part = dot(pick, hid_part, 1, 0).astype(BF16)
    hidden = gather_small(hid_part).transpose(1, 0, 2).reshape(hid_part.shape[0], hid_count)
    core = lax.axis_index("core")
    order = jnp.arange(chips * part, dtype=jnp.int32)
    base_row = (order // part) * (2 * part) + order % part
    every = jnp.arange(rows, dtype=jnp.int32)[None, :]
    own_pick = (base_row[:, None] + core * part == every).astype(BF16)
    sib_pick = (base_row[:, None] + (1 - core) * part == every).astype(BF16)
    late_cot, hidden = lax.optimization_barrier((cotangent, hidden))
    cot_own = dot(own_pick, late_cot, 1, 0).astype(BF16)
    cot_sib = dot(sib_pick, late_cot, 1, 0).astype(BF16)
    theirs = dot(cot_sib, w_query, 1, 1).astype(BF16)
    swapped = lax.ppermute(theirs, "core", [(0, 1), (1, 0)])
    mine = (dot(cot_own, w_query, 1, 1) + swapped.astype(F32)).astype(BF16)
    reduced = lax.psum_scatter(mine, "z", scatter_dimension=0, tiled=True)
    gen_a = dot(hidden, head_a.reshape(hid_count, width), 1, 0).astype(BF16)
    gen_b = dot(hidden, head_b.reshape(hid_count, width), 1, 0).astype(BF16)
    factors = lax.all_to_all(jnp.stack([gen_a, gen_b], 1), "dp", 0, 0, tiled=True)
    down_w = factors[:, 0]
    up_w = factors[:, 1]
    rank = down_w.shape[0]
    back_part = dot(up_w, cotangent, 1, 1).astype(BF16)
    both = gather_small(jnp.concatenate([down_w, back_part], 0))
    back_low = both[:, rank:].astype(F32).sum(0).astype(BF16)
    full_a = both[:, :rank].transpose(1, 0, 2).reshape(rank, -1)

    down_low = dot(whole, full_a, 1, 1).astype(BF16)
    columns = lax.dynamic_slice_in_dim(whole, shard * width, width, 1)
    scale = 1.0 / rows
    grad_a = (dot(back_low, columns, 1, 0) * scale).astype(BF16)
    grad_b = (dot(down_low, cotangent, 0, 0) * scale).astype(BF16)
    own = lax.all_to_all(jnp.stack([grad_a, grad_b], 1), "dp", 0, 0, tiled=True)
    head_grad_a = dot(hidden, own[:, 0], 0, 0).astype(BF16).reshape(hid_count, rank_rows, width)
    head_grad_b = dot(hidden, own[:, 1], 0, 0).astype(BF16).reshape(hid_count, rank_rows, width)
    output = (dot(whole, w_query, 1, 0) + dot(down_low, up_w, 1, 0)).astype(BF16)
    back_low, output, head_grad_a, head_grad_b = lax.optimization_barrier(
        (back_low, output, head_grad_a, head_grad_b)
    )
    back_rows = lax.dynamic_slice_in_dim(back_low, shard * part, part, 1)
    grad_tokens = (dot(back_rows, full_a, 0, 0) + reduced.astype(F32)).astype(BF16)
    return (output, grad_tokens, head_grad_a, head_grad_b)


def solution(mesh):
    dp, tensor = mesh.devices.shape
    small = Mesh(mesh.devices.reshape(dp, tensor // 2, 2), ("dp",) + AXIS)
    return jax.shard_map(
        local,
        mesh=small,
        in_specs=(
            P(("dp",) + AXIS, None),
            P(None, AXIS),
            P("dp", AXIS),
            P(),
            P(None, AXIS),
            P(None, "dp", AXIS),
            P(None, "dp", AXIS),
            P(),
        ),
        out_specs=(
            P("dp", AXIS),
            P(("dp",) + AXIS, None),
            P(None, "dp", AXIS),
            P(None, "dp", AXIS),
        ),
        check_vma=False,
    )
```

time: 159 us -> 133 us (0.84)
  blocking collectives: 38.5 us -> 13.6 us
  matrix products: 47.3 us -> 41.9 us
  waiting for transfers between devices: 42.3 us -> 38.7 us
  starting transfers between devices: 14.8 us -> 17.1 us
  other arithmetic: 0.06 us -> 2 us
    reduce_scatter x1, waiting for transfers between devices: 41.6 us -> 0.03 us  [local(): reduced = lax.psum_scatter(mine, 'z', scatter_dimension=0, tiled=True)]
    all_gather x2 -> x0, blocking collectives: 38.5 us -> none  [the longest x1 20.1 us: local(): hidden = lax.all_gather(hid_part, 'tensor', axis=1, tiled=True)]
    all_to_all x1 -> x2, waiting for transfers between devices: 0.01 us -> 29.8 us  [gather_small(): lax.all_to_all(jnp.broadcast_to(x[None], (n,) + x.shape), AXIS, 0, 0, til...]
    all_to_all x0 -> x1, blocking collectives: none -> 13.6 us  [local(): lax.all_to_all(jnp.stack([gen_a, gen_b], 1), 'dp', 0, 0, tiled=True)]
    ppermute x0 -> x1, waiting for transfers between devices: none -> 8.19 us  [local(): swapped = lax.ppermute(theirs, 'core', [(0, 1), (1, 0)])]
    dot_general x13 -> x14, matrix products: 47.3 us -> 41.9 us  [dot(): lax.dot_general(a, b, (((ca,), (cb,)), ((), ())), preferred_element_type=...]
    all_to_all x1 -> x2, starting transfers between devices: 7.48 us -> 12.1 us  [gather_small(): lax.all_to_all(jnp.broadcast_to(x[None], (n,) + x.shape), AXIS, 0, 0, til...]
    all_to_all x1, starting transfers between devices: 7.27 us -> 4.77 us  [local(): own = lax.all_to_all(jnp.stack([grad_a, grad_b], 1), 'dp', 0, 0, tiled=True)]
  transfers between devices with their start and end apart: 4 -> 6, of which waited for: 1 -> 3; matrix products, arithmetic and copies ran while one was open for 31% -> 34% of each run, Pallas kernels for 0% -> 0%
where the time goes in v2:
time: 133 us; the launch traced here: 132 us
  matrix products  41.9 us (32%)
  waiting for transfers between devices  38.7 us (29%)
  starting transfers between devices  17.1 us (13%)
  between operations  15.6 us (12%)
  blocking collectives  13.6 us (10%)
  local copies, waits for them, and re-layouts  2.69 us (2%)
  other arithmetic  2 us (2%)
    dot_general x14, matrix products, dot(): lax.dot_general(a, b, (((ca,), (cb,)), ((), ())), preferred_element_type=...  41.9 us
    all_to_all x2, waiting for transfers between devices, gather_small(): lax.all_to_all(jnp.broadcast_to(x[None], (n,) + x.shape), AXIS, 0, 0, til...  29.8 us
    all_to_all x1, blocking collectives, local(): lax.all_to_all(jnp.stack([gen_a, gen_b], 1), 'dp', 0, 0, tiled=True)  13.6 us
    all_to_all x2, starting transfers between devices, gather_small(): lax.all_to_all(jnp.broadcast_to(x[None], (n,) + x.shape), AXIS, 0, 0, til...  12.1 us
    ppermute x1, waiting for transfers between devices, local(): swapped = lax.ppermute(theirs, 'core', [(0, 1), (1, 0)])  8.19 us
    all_to_all x1, starting transfers between devices, local(): own = lax.all_to_all(jnp.stack([grad_a, grad_b], 1), 'dp', 0, 0, tiled=True)  4.77 us
  transfers between devices with their start and end apart: 6, of which 3 were waited for; matrix products, arithmetic and copies ran while one was open for 34% of the time, Pallas kernels for 0%

profile of v2, /device:TPU:2, one launch (start us, length us, event | category | flops | bytes accessed | tf_op | source)
XLA Modules:
  0.0 131.7 jit_solution(7355921292236708101)
XLA Ops:
  8.0 0.0 copy-start
  8.0 0.0 all-gather.2.cloned.1.call-start
  8.1 0.7 all-gather.2.cloned.1.call-update
  8.7 1.3 convolution_convert_fusion.9
  10.0 0.7 reshape.63
  10.8 8.6 %all-to-all-start = ((bf16[16,2,256]{2,1,0:T(2,128)(2,1)}), bf16[16,2,256]{2,1,0:T(2,128)(2,1)S(1)}, u32[]{:S(2)}, u32[]{:S(2)}) async-start(bf16[16,2,256]{2,1,0:T(2,128)(2,1)} %reshape.63), calls=%async_computation | async-start | bytes 32768 | tf_op jit(solution)/shard_map/all_to_all | solution.py:18
  19.3 0.0 reduce-scatter.2.cloned.1.call-start
  19.4 7.6 %all-to-all-done = bf16[16,2,256]{2,1,0:T(2,128)(2,1)S(1)} async-done(((bf16[16,2,256]{2,1,0:T(2,128)(2,1)}), bf16[16,2,256]{2,1,0:T(2,128)(2,1)S(1)}, u32[]{:S(2)}, u32[]{:S(2)}) %all-to-all-start) | async-done | bytes 16416 | tf_op jit(solution)/shard_map/all_to_all | solution.py:18
  27.0 0.1 reshape.64
  27.1 0.1 reshape.57
  27.2 0.0 copy-done
  27.2 8.0 %convolution_convert_fusion = bf16[256,8192]{1,0:T(8,128)(2,1)} fusion(bf16[8192,512]{1,0:T(8,128)(2,1)} %param.9, bf16[512,512]{1,0:T(8,128)(2,1)S(1)} %copy-done, s32[256]{0:T(256)S(1)} %broadcast_add_fusion), kind=kOutput, calls=%fused_computation | convolution fusion | flops 2284060672 | bytes 13108224 | tf_op jit(solution)/shard_map/dot_general | solution.py:13
  35.2 0.1 collective-permute-start
  35.3 0.0 copy-start.1
  35.3 0.0 copy-start.2
  35.3 8.2 %collective-permute-done = bf16[256,8192]{1,0:T(8,128)(2,1)} collective-permute-done((bf16[256,8192]{1,0:T(8,128)(2,1)}, bf16[256,8192]{1,0:T(8,128)(2,1)}, u32[]{:S(2)}, u32[]{:S(2)}) %collective-permute-start) | collective-permute-done | bytes 4194336 | tf_op jit(solution)/shard_map/ppermute | solution.py:45
  43.5 11.6 %add_convert_fusion = bf16[256,8192]{1,0:T(8,128)(2,1)} fusion(bf16[256,8192]{1,0:T(8,128)(2,1)} %collective-permute-done, bf16[8192,512]{1,0:T(8,128)(2,1)} %param.9, bf16[512,512]{1,0:T(8,128)(2,1)S(1)} %copy-done, s32[256]{0:T(256)S(1)} %broadcast_add_fusion.1), kind=kOutput, calls=%fused_computation.1 | convolution fusion | flops 2288254976 | bytes 17302528 | tf_op jit(solution)/shard_map/dot_general | solution.py:13
  55.1 0.0 reduce-scatter.2.cloned.1.call-update
  55.1 0.0 copy-done.1
  55.2 0.2 fusion.6
  55.3 0.0 copy-done.2
  55.3 0.2 fusion.7
  55.6 13.6 %all_to_all.20 = bf16[16,2,512]{2,1,0:T(2,128)(2,1)S(1)} all-to-all(bf16[16,2,512]{2,1,0:T(2,128)(2,1)S(1)} %copy.18), channel_id=1, replica_groups=mesh['dp'=16,'z'=8,'core'=2] {'dp'}, dimensions={0} | all-to-all | bytes 65536 | tf_op jit(solution)/shard_map/all_to_all | solution.py:50
  69.3 0.2 convolution_convert_fusion.6
  69.5 0.9 broadcast_in_dim.5
  70.4 3.6 %all-to-all-start.2 = ((bf16[16,32,512]{2,1,0:T(8,128)(2,1)}), bf16[16,32,512]{2,1,0:T(8,128)(2,1)S(1)}, u32[]{:S(2)}, u32[]{:S(2)}) async-start(bf16[16,32,512]{2,1,0:T(8,128)(2,1)} %broadcast_in_dim.5), calls=%async_computation.2 | async-start | bytes 1048576 | tf_op jit(solution)/shard_map/all_to_all | solution.py:18
  74.0 22.2 %all-to-all-done.2 = bf16[16,32,512]{2,1,0:T(8,128)(2,1)S(1)} async-done(((bf16[16,32,512]{2,1,0:T(8,128)(2,1)}), bf16[16,32,512]{2,1,0:T(8,128)(2,1)S(1)}, u32[]{:S(2)}, u32[]{:S(2)}) %all-to-all-start.2) | async-done | bytes 524320 | tf_op jit(solution)/shard_map/all_to_all | solution.py:18
  96.2 0.0 all-gather.2.cloned.1.call-done
  96.3 1.2 fusion.9
  97.5 5.7 %convolution_convert_fusion.5 = bf16[16,512]{1,0:T(8,128)(2,1)S(1)} fusion(bf16[16,8192]{1,0:T(8,128)(2,1)S(1)} %bitcast.56, bf16[512,8192]{1,0:T(8,128)(2,1)} %all-gather.2.cloned.1.call-done), kind=kOutput, calls=%fused_computation.13 | convolution fusion | flops 134225920 | bytes 8667136 | tf_op jit(solution)/shard_map/dot_general | solution.py:13
  103.2 0.2 fusion.8
  103.4 0.7 copy.22
  104.1 4.8 %all-to-all-start.3 = ((bf16[16,2,512]{2,1,0:T(2,128)(2,1)}), bf16[16,2,512]{2,1,0:T(2,128)(2,1)S(1)}, u32[]{:S(2)}, u32[]{:S(2)}) async-start(bf16[16,2,512]{2,1,0:T(2,128)(2,1)} %copy.22), calls=%async_computation.3 | async-start | bytes 65536 | tf_op jit(solution)/shard_map/all_to_all | solution.py:64
  108.9 9.6 %fusion.31 = f32[512,512]{1,0:T(8,128)S(1)} fusion(bf16[512,8192]{1,0:T(8,128)(2,1)} %all-gather.2.cloned.1.call-done, bf16[8192,512]{1,0:T(8,128)(2,1)} %param.9), kind=kOutput, calls=%fused_computation.63 | convolution fusion | flops 4294967296 | bytes 17825792 | tf_op jit(solution)/shard_map/dot_general | solution.py:13
  118.5 1.1 fusion
  119.6 0.0 all-to-all-done.3
  119.6 1.1 fusion.1
  120.7 1.1 fusion.2
  121.9 0.4 fusion.17
  122.2 0.0 reduce-scatter.2.cloned.1.call-done
  122.3 1.9 %add_convert_fusion.1 = bf16[32,8192]{1,0:T(8,128)(2,1)} fusion(f32[32,8192]{1,0:T(8,128)S(1)} %fusion.17, bf16[32,8192]{1,0:T(8,128)(2,1)} %reduce-scatter.2.cloned.1.call-done), kind=kLoop, calls=%fused_computation.24 | loop fusion | flops 786432 | bytes 2097152 | tf_op jit(solution)/shard_map/convert_element_type | solution.py:72
  (13 shorter events, 0.3 us)
Async XLA Ops:
  8.0 19.2 %copy-start = (bf16[512,512]{1,0:T(8,128)(2,1)S(1)}, bf16[512,512]{1,0:T(8,128)(2,1)}, u32[]{:S(2)}) copy-start(bf16[512,512]{1,0:T(8,128)(2,1)} %param.10) | copy-start | bytes 1572868
  8.0 88.2 %all-gather.2.cloned.1.call-start = ((), (), s32[]{:S(2)}) async-start(), calls=%async_computation.5 | async-start | bytes 8912896 | tf_op jit(solution)/shard_map/all_gather | solution.py:30
  10.8 16.2 %all-to-all-start = ((bf16[16,2,256]{2,1,0:T(2,128)(2,1)}), bf16[16,2,256]{2,1,0:T(2,128)(2,1)S(1)}, u32[]{:S(2)}, u32[]{:S(2)}) async-start(bf16[16,2,256]{2,1,0:T(2,128)(2,1)} %reshape.63), calls=%async_computation | async-start | bytes 32768 | tf_op jit(solution)/shard_map/all_to_all | solution.py:18
  19.3 102.9 %reduce-scatter.2.cloned.1.call-start = ((), (), s32[]{:S(2)}) async-start(), calls=%async_computation.6 | async-start | bytes 4718592 | tf_op jit(solution)/shard_map/reduce_scatter | solution.py:47
  35.2 8.3 %collective-permute-start = (bf16[256,8192]{1,0:T(8,128)(2,1)}, bf16[256,8192]{1,0:T(8,128)(2,1)}, u32[]{:S(2)}, u32[]{:S(2)}) collective-permute-start(bf16[256,8192]{1,0:T(8,128)(2,1)} %convolution_convert_fusion), channel_id=1, source_target_pairs={{0,1},{1,0},{2,3},{3,2},{4,5},{5,4},{6,7},{7,6},{8,9},{9,8},{10,11... | collective-permute-start | bytes 12582920 | tf_op jit(solution)/shard_map/ppermute | solution.py:45
  35.3 19.8 %copy-start.1 = (bf16[512,1,512]{2,0,1:T(8,128)(2,1)S(1)}, bf16[512,1,512]{2,0,1:T(8,128)(2,1)}, u32[]{:S(2)}) copy-start(bf16[512,1,512]{2,0,1:T(8,128)(2,1)} %param.13) | copy-start | bytes 1572868
  35.3 20.0 %copy-start.2 = (bf16[512,1,512]{2,0,1:T(8,128)(2,1)S(1)}, bf16[512,1,512]{2,0,1:T(8,128)(2,1)}, u32[]{:S(2)}) copy-start(bf16[512,1,512]{2,0,1:T(8,128)(2,1)} %param.14) | copy-start | bytes 1572868
  70.4 25.8 %all-to-all-start.2 = ((bf16[16,32,512]{2,1,0:T(8,128)(2,1)}), bf16[16,32,512]{2,1,0:T(8,128)(2,1)S(1)}, u32[]{:S(2)}, u32[]{:S(2)}) async-start(bf16[16,32,512]{2,1,0:T(8,128)(2,1)} %broadcast_in_dim.5), calls=%async_computation.2 | async-start | bytes 1048576 | tf_op jit(solution)/shard_map/all_to_all | solution.py:18
  104.1 15.5 %all-to-all-start.3 = ((bf16[16,2,512]{2,1,0:T(2,128)(2,1)}), bf16[16,2,512]{2,1,0:T(2,128)(2,1)S(1)}, u32[]{:S(2)}, u32[]{:S(2)}) async-start(bf16[16,2,512]{2,1,0:T(2,128)(2,1)} %copy.22), calls=%async_computation.3 | async-start | bytes 65536 | tf_op jit(solution)/shard_map/all_to_all | solution.py:64
Sparse Core Ops, SparseCore 0:
  10.6 60.2 all-gather.1
Sparse Core Ops, SparseCore 1:
  55.2 64.1 reduce-scatter.1
